TPU v7x, 512 devices: a whole 4x8x8 slice. The times are simulated.
512 devices in a mesh: gx: 8 (over x, core), gy: 8 (over y), obs: 8 (over z).
Axes of the slice: x: 4, y: 8, z: 8, core: 2. Of those that a mesh axis runs over, the one named last changes fastest.
Arguments:
- control: float32 [4, 8, 1024, 1024], P(None, 'obs', 'gy', 'gx'), may hold values from -6 to 6
- diffusivity: float32 [2, 8, 1024, 1024], P(None, 'obs', 'gy', 'gx'), may hold values from 0.12 to 0.245
- prof_tile: int32 [32768, 1], P(('gx', 'gy')), may hold values from 0 to 63; in each aligned block of 512 rows (0 to 511, 512 to 1023, ...) at most 16 rows name the same one
- prof_cell: int32 [32768], P(('gx', 'gy')), may hold values from 0 to 16383
- obs_prof: int32 [262144], P(('gx', 'gy', 'obs')), may hold values from 0 to 511
- obs_field: int32 [262144], P(('gx', 'gy', 'obs')), may hold values from 0 to 3
- obs_level: int32 [262144], P(('gx', 'gy', 'obs')), may hold values from 0 to 6
- obs_weight: float32 [262144], P(('gx', 'gy', 'obs')), may hold values from 0 to 1
- innovation: float32 [262144], P(('gx', 'gy', 'obs')), may hold values from -6 to 6
- obs_precision: float32 [262144], P(('gx', 'gy', 'obs')), may hold values from 0.25 to 4
Outputs:
- gradient: float32 [4, 8, 1024, 1024], P(None, 'obs', 'gy', 'gx')
- departures: float32 [262144], P(('gx', 'gy', 'obs'))
Inputs may be any that keep to these rules, and one draw needn't show every extreme that they name: `prof_tile`: in each aligned block of 512 rows (the profiles of one tile) no tile is named by more than 16 rows; in some blocks one tile is named by exactly 16 rows.
All inputs are finite; a program needn't handle non-finite values.
Results may differ from a plain program's by a relative error of at most 0.00002.
Values sent between devices are 32-bit elements; how exact they have to be, the bound alone decides.
No kernel may reach another device: no remote copies, remote signals or barrier semaphores. Data moves between devices by JAX's collectives and lax.ppermute only.
A program may use at most 64 MiB of HBM per device.

v0:
```python
import jax
import jax.numpy as jnp
from jax import lax
from jax.experimental import pallas as pl
from jax.experimental.pallas import tpu as pltpu
from jax.sharding import PartitionSpec as P


STEPS = 10
HALO = STEPS
ROWS = 16
EAST_AT, NORTH_AT = HALO, 74
PAD = 8
F32, BF16, I32 = jnp.float32, jnp.bfloat16, jnp.int32


def lanes(shape):
    return lax.broadcasted_iota(I32, shape, len(shape) - 1)


def subs(shape):
    return lax.broadcasted_iota(I32, shape, len(shape) - 2)


def split3(x):
    hi = x.astype(BF16)
    rest = x - hi.astype(F32)
    mid = rest.astype(BF16)
    low = (rest - mid.astype(F32)).astype(BF16)
    return hi, mid, low


def one_hot(flags):
    return jnp.where(flags, 1.0, 0.0).astype(BF16)


def dot_nn(a, b):
    return lax.dot_general(a, b, (((1,), (0,)), ((), ())), preferred_element_type=F32)


def dot_nt(a, b):
    return lax.dot_general(a, b, (((1,), (1,)), ((), ())), preferred_element_type=F32)


def call(body, outs, args, scratch=(), flops=1_000_000, hbm=False):
    vmem = pl.BlockSpec(memory_space=pltpu.VMEM)
    given = pl.BlockSpec(memory_space=pltpu.HBM) if hbm else vmem
    outs = [o if isinstance(o, jax.ShapeDtypeStruct) else jax.ShapeDtypeStruct(o, F32) for o in outs]
    return pl.pallas_call(
        body,
        out_shape=outs,
        in_specs=[given] * len(args),
        out_specs=[vmem] * len(outs),
        scratch_shapes=list(scratch),
        cost_estimate=pl.CostEstimate(
            flops=flops,
            bytes_accessed=sum(4 * x.size for x in (*args, *outs)),
            transcendentals=0,
        ),
        compiler_params=pltpu.CompilerParams(vmem_limit_bytes=16 << 20),
    )(*args)


def mask_north(rate_ref):
    last = rate_ref.shape[1] - 8
    rows = rate_ref[1, pl.ds(last, 8), :]
    top = lax.axis_index("gy") == lax.axis_size("gy") - 1
    rate_ref[1, pl.ds(last, 8), :] = jnp.where(top & (subs(rows.shape) == 7), 0.0, rows)


def offset(f, planes, width):
    return f * (width // planes)


def turn(x, by):
    by %= x.shape[-1]
    return pltpu.roll(x, by, x.ndim - 1) if by else x


def within(shape, low):
    width = shape[-1]
    return ((lanes(shape) - low % width + width) & (width - 1)) < HALO


def pack_edges(turned, rates, east_ref, west_ref):
    shape = turned[0].shape
    width = shape[-1]
    east = west = jnp.zeros(shape, F32)
    for f, x in enumerate(turned):
        low = offset(f, len(turned), width)
        east = jnp.where(within(shape, low - HALO), x, east)
        west = jnp.where(within(shape, low), x, west)
    for at, x in rates:
        east = jnp.where(within(shape, at), turn(x, at + HALO - width), east)
        west = jnp.where(within(shape, at + 32), turn(x, at + 32), west)
    east_ref[...] = east
    west_ref[...] = west


def pack_inputs(*refs):
    sources, (east, west, obs, turned), kept, (ctl, sems) = refs[:10], refs[10:14], refs[14:23], refs[23:]
    copies = [
        pltpu.make_async_copy(source, target, sems.at[i])
        for i, (source, target) in enumerate(zip(sources, (ctl, *kept)))
    ]
    for copy in copies:
        copy.start()
    for copy in copies:
        copy.wait()
    rate, _, _, prof, field, level, weight, innov, prec = kept
    mask_north(rate)
    fields = ctl.shape[0]
    planes = [turn(ctl[f], offset(f, fields, ctl.shape[2])) for f in range(fields)]
    for f in range(fields):
        turned[f] = planes[f]
    pack_edges(planes, ((EAST_AT, rate[0]), (NORTH_AT, rate[1])), east, west)
    index = ((field[...] * 8 + level[...]) * 512 + prof[...]).astype(F32)
    rows = jnp.concatenate([index, weight[...], innov[...], prec[...]], axis=0)
    for z in range(obs.shape[0] // rows.shape[0]):
        obs[pl.ds(z * rows.shape[0], rows.shape[0]), :] = rows


def odd():
    return lax.rem(lax.axis_index("gy"), 2)


def pick(first, second):
    return pl.multiple_of(jnp.where(odd() == 0, first, second), 8)


def meet(refs, strip, first, second):
    last = strip.shape[0] - ROWS
    for target, at in ((first, pick(last, 0)), (second, pick(0, last))):
        for a, ref in enumerate(refs + [strip]):
            target[a] = ref[pl.ds(at, ROWS), :]


def edges_first(own, rate, left, right, strip, first, second):
    strip[...] = left[...] + right[...]
    refs = [own.at[f] for f in range(own.shape[0])] + [rate.at[0], rate.at[1]]
    meet(refs, strip, first, second)


def edges_second(pulled, left, right, strip, first, second):
    strip[...] = left[...] + right[...]
    meet([pulled.at[f] for f in range(pulled.shape[0])], strip, first, second)


def blocks(own, first, second):
    low, high = PAD, PAD + ROWS + own.shape[0]
    return ((pick(high, low), first), (PAD + ROWS, own), (pick(low, high), second))


def one_step(source, target, coef):
    fields = source.shape[0] - 1
    width = source.shape[2]
    for tile in range(coef.shape[0]):
        row = PAD + 8 * tile
        here, up, down = pl.ds(row, 8), pl.ds(row + 1, 8), pl.ds(row - 1, 8)
        lane = lanes((8, width))

        def new(p, v, east, west):
            c = [coef[tile, 5 * p + i] for i in range(5)]
            total = c[0] * v + c[1] * east + c[2] * west
            target[p, here, :] = total + c[3] * source[p, up, :] + c[4] * source[p, down, :]

        strip = source[fields, here, :]
        strip_east = next_east = turn(strip, -1)
        strip_west = next_west = turn(strip, 1)
        for f in range(fields):
            v = source[f, here, :]
            start = lane == offset(f, fields, width)
            stop = lane == (offset(f, fields, width) - 1) % width
            east, west = turn(v, -1), turn(v, 1)
            next_east = jnp.where(stop, east, next_east)
            next_west = jnp.where(start, west, next_west)
            new(f, v, jnp.where(stop, strip_east, east), jnp.where(start, strip_west, west))
        new(fields, strip, next_east, next_west)


def ten_steps(a, b, coef):
    def body(_):
        one_step(a, b, coef)
        one_step(b, a, coef)

    each(STEPS // 2, body)


def each(count, body):
    def step(i, carry):
        body(i)
        return carry

    lax.fori_loop(0, count, step, 0)


def rows_at(start, size):
    return pl.ds(pl.multiple_of(start, 8), size)


def clear_ends(a):
    clear = jnp.zeros((PAD, a.shape[2]), F32)
    for plane in range(a.shape[0]):
        a[plane, pl.ds(0, PAD), :] = clear
        a[plane, pl.ds(a.shape[1] - PAD, PAD), :] = clear


def load_field(a, b, own, strip, first, second, packed):
    fields = own.shape[0]
    for f in range(fields):
        for row, block in blocks(own[f], first[f], second[f]):
            a[f, pl.ds(row, block.shape[0]), :] = block
    for row, block in blocks(strip[...], first[packed], second[packed]):
        a[fields, pl.ds(row, block.shape[0]), :] = block
    clear_ends(a)
    clear_ends(b)


def rate_strip(packed, at, fields):
    shape = packed.shape
    width = shape[-1]
    east = turn(packed, -at - 32)
    west = turn(packed, width - HALO - at)
    g = jnp.where(within(shape, 0), east, jnp.where(within(shape, -HALO), west, 0.0))
    by = width // fields
    while by < width:
        g = g + turn(g, by)
        by *= 2
    return g


def diffuse_control(own, rate, strip, first, second, inc, coef, a, b, wide, north):
    fields, height, width = own.shape
    load_field(a, b, own, strip, first, second, fields + 2)
    for k in range(2):
        for row, block in blocks(rate[k], first[fields + k], second[fields + k]):
            wide[k, pl.ds(row, block.shape[0]), :] = block
    north[:, pl.ds(0, PAD), :] = jnp.zeros((fields + 1, PAD, width), F32)
    size = 80

    def turned(block):
        here = rows_at(PAD + size * block, size)
        n = wide[1, here, :]
        for f in range(fields):
            north[f, here, :] = turn(n, offset(f, fields, width))
        north[fields, here, :] = rate_strip(a[fields, here, :], NORTH_AT, fields)
        for k in range(size // 8):
            tile = size // 8 * block + k
            e = wide[0, rows_at(PAD + 8 * tile, 8), :]
            beyond = rate_strip(a[fields, rows_at(PAD + 8 * tile, 8), :], EAST_AT, fields)
            before = strip_before = turn(beyond, 1)
            lane = lanes((8, width))
            planes = []
            for f in range(fields):
                low = offset(f, fields, width)
                start = lane == low
                moved = turn(e, low + 1)
                strip_before = jnp.where(start, moved, strip_before)
                planes.append((turn(e, low), jnp.where(start, before, moved)))
            planes.append((beyond, strip_before))
            for p, (east, west) in enumerate(planes):
                both = north[p, rows_at(8 * tile, 16), :]
                n, s = both[8:], both[7:15]
                for i, value in enumerate((1.0 - east - west - n - s, east, west, n, s)):
                    coef[tile, 5 * p + i] = value

    each(coef.shape[0] * 8 // size, turned)
    ten_steps(a, b, coef)
    size = 64

    def back(block):
        for f in range(fields):
            value = a[f, rows_at(PAD + ROWS + size * block, size), :]
            inc[f, rows_at(size * block, size), :] = turn(value, -offset(f, fields, width))

    each(height // size, back)


def diffuse_pulled(pulled, strip, first, second, coef, own, grad, a, b):
    fields, height, width = pulled.shape
    load_field(a, b, pulled, strip, first, second, fields)
    ten_steps(a, b, coef)
    size = 64

    def back(block):
        for f in range(fields):
            here = rows_at(size * block, size)
            total = own[f, here, :] + a[f, rows_at(PAD + ROWS + size * block, size), :]
            grad[f, here, :] = turn(total, -offset(f, fields, width))

    each(height // size, back)


def tables(obs, holder, cell, out, slots):
    profiles = holder.shape[1]
    level_here = lax.axis_index("obs")
    groups = obs.shape[0] // 16
    width = obs.shape[1]
    acc = jnp.zeros((48, profiles), F32)
    row16 = subs((16, width))
    for z in range(groups):
        parts = ([], [], [])
        hots = []
        for c in range(4):
            at = 16 * z + c
            index = obs[pl.ds(at, 1), :].astype(I32)
            w, y, q = (obs[pl.ds(at + 4 * k, 1), :] for k in (1, 2, 3))
            prof = index & 511
            level = (index >> 9) & 7
            field = index >> 12
            low = jnp.where(level == level_here, q, 0.0)
            high = jnp.where(level == level_here - 1, q, 0.0)
            v = 1.0 - w
            lw, hv = low * w, high * v
            rows = (lw * w + hv * v, lw * v, hv * w, (lw + hv) * y)
            value = jnp.where(
                row16 < 8,
                jnp.where(row16 < 4, rows[0], rows[1]),
                jnp.where(row16 < 12, rows[2], rows[3]),
            )
            value = jnp.where((row16 & 3) == field, value, 0.0)
            for part, x in zip(parts, split3(value)):
                part.append(x)
            hots.append(one_hot(subs((profiles, width)) == prof))
        left = jnp.concatenate([jnp.concatenate(p, axis=1) for p in parts], axis=0)
        acc = acc + dot_nt(left, jnp.concatenate(hots, axis=1))
    table = acc[0:16] + acc[16:32] + acc[32:48]
    held = subs((out.shape[0], profiles)) == holder[...]
    held16 = one_hot(held)
    before = one_hot(subs((profiles, profiles)) < lanes((profiles, profiles)))
    slot = jnp.sum(jnp.where(held, dot_nn(held16, before), 0.0), axis=0, keepdims=True)
    slots[...] = slot
    place = slot.astype(I32)
    cells = cell[...].astype(F32)
    mine = [subs((8, profiles)) * 2 + k == place for k in range(2)]
    for k in range(2):
        value = jnp.concatenate(
            [jnp.where(mine[k], table[r : r + 1], 0.0) for r in range(16)], axis=0
        )
        total = sum(dot_nt(held16, part) for part in split3(value))
        out[:, 0, pl.ds(128 * k, 128)] = total
    value = jnp.concatenate(
        [jnp.where(mine[k], cells, 0.0) for k in range(2)]
        + [jnp.zeros((112, profiles), F32)],
        axis=0,
    )
    out[:, 0, pl.ds(256, 128)] = sum(dot_nt(held16, part) for part in split3(value)[:2])


def gather(inc, sent, found, tab, hold):
    fields = inc.shape[0]
    tab[pl.ds(0, 128), :] = jnp.concatenate([sent[:, 0, pl.ds(0, 128)], sent[:, 0, pl.ds(128, 128)]], axis=0).T
    cells = sent[:, 0, pl.ds(256, 128)]
    cells = jnp.concatenate([cells, cells], axis=0).T
    cells = jnp.where(lanes((8, 128)) < 64, cells[0:8], cells[8:16])
    tab[pl.ds(128, 8), :] = cells
    cells = cells.astype(I32)
    left = jnp.concatenate(
        [jnp.concatenate(split3(inc[f]), axis=1) for f in range(fields)], axis=0
    )
    for pair in range(4):
        hots, lats = [], []
        for s in (2 * pair, 2 * pair + 1):
            row = cells[s : s + 1]
            hots.append(one_hot(subs((128, 128)) == (row & 127)))
            lats.append(subs((128, 128)) == (row >> 7))
        hot = jnp.concatenate(hots, axis=1)
        hit = dot_nn(left, jnp.concatenate([hot, hot, hot], axis=0))
        for f in range(fields):
            for i in range(2):
                part = hit[128 * f : 128 * (f + 1), 128 * i : 128 * (i + 1)]
                hold[pl.ds(8 * f + 2 * pair + i, 1), :] = jnp.sum(
                    jnp.where(lats[i], part, 0.0), axis=0, keepdims=True
                )
    rows = hold[...]
    for z in range(found.shape[0] // rows.shape[0]):
        found[pl.ds(z * rows.shape[0], rows.shape[0]), :] = rows


def scatter(levels, tab, pulled, east, west, columns):
    fields = pulled.shape[0]
    rows = 8 * fields
    here = lax.axis_index("obs")
    top = levels.shape[0] // rows - 1

    def level(k):
        return levels[pl.ds(pl.multiple_of(jnp.clip(k, 0, top) * rows, rows), rows), :]

    own, above, below = level(here), level(here + 1), level(here - 1)
    d, o, u, b = (tab[pl.ds(rows * k, rows), :] for k in range(4))
    amount = d * own + o * above + u * below - b
    cells = tab[pl.ds(4 * rows, 8), :].astype(I32)
    lat = [subs((128, 128)) == (cells[s : s + 1] >> 7) for s in range(8)]
    hot = jnp.concatenate(
        [one_hot(subs((128, 128)) == (cells[s : s + 1] & 127)) for s in range(8)], axis=1
    )
    planes = []
    for f in range(fields):
        total = jnp.zeros((128, 128), F32)
        for part in split3(amount[8 * f : 8 * f + 8]):
            wide = part.astype(F32)
            left = jnp.concatenate(
                [jnp.where(lat[s], wide[s : s + 1], 0.0).astype(BF16) for s in range(8)], axis=1
            )
            total = total + dot_nt(left, hot)
        planes.append(turn(total, offset(f, fields, 128)))
        pulled[f] = planes[f]
    pack_edges(planes, (), east, west)
    for half in range(2):
        turned_block = levels[pl.ds(128 * half, 128), :].T
        for k in range(2):
            columns[:, 2 * k + half, :] = turned_block[64 * k : 64 * (k + 1)]


def depart(columns, holder, slots, prof, field, level, weight, innov, prec, out):
    profiles = holder.shape[1]
    left = jnp.concatenate(
        [
            jnp.concatenate([columns[:, half, :], columns[:, 2 + half, :]], axis=0).T
            for half in range(2)
        ],
        axis=0,
    )
    place = slots[...].astype(I32)
    row = subs((128, profiles))
    held = one_hot(((row & 63) == holder[...]) & ((row >> 6) == (place & 1)))
    spread = dot_nn(
        jnp.concatenate(split3(left), axis=1), jnp.concatenate([held, held, held], axis=0)
    )
    mine = subs((8, profiles)) == (place >> 1)
    values = jnp.concatenate(
        [
            jnp.sum(jnp.where(mine, spread[8 * r : 8 * r + 8], 0.0), axis=0, keepdims=True)
            for r in range(32)
        ],
        axis=0,
    )
    hot = jnp.concatenate(
        [one_hot(subs((profiles, 128)) == prof[pl.ds(c, 1), :]) for c in range(4)], axis=1
    )
    seen = sum(dot_nn(part, hot) for part in split3(values))
    row = subs((32, 128))
    for c in range(4):
        at = pl.ds(c, 1)
        code = level[at, :] * 4 + field[at, :]
        part = seen[:, 128 * c : 128 * (c + 1)]
        low = jnp.sum(jnp.where(row == code, part, 0.0), axis=0, keepdims=True)
        high = jnp.sum(jnp.where(row == code + 4, part, 0.0), axis=0, keepdims=True)
        w = weight[at, :]
        out[at, :] = prec[at, :] * (w * low + (1.0 - w) * high - innov[at, :])


def ring(axis, by):
    count = lax.axis_size(axis)
    return [(i, (i + by) % count) for i in range(count)]


def pair(forward, back, axis):
    return (
        lax.ppermute(forward, axis, ring(axis, 1)),
        lax.ppermute(back, axis, ring(axis, -1)),
    )


def swap(first, second, axis):
    count = lax.axis_size(axis)
    low = [(i, i ^ 1) for i in range(count)]
    high = [(i, (i + 1 ^ 1) - 1) for i in range(1, count - 1)]
    first = lax.ppermute(first, axis, low)
    second = lax.ppermute(second, axis, high)
    return first, second


def exchange(x, axes):
    return lax.all_to_all(x, axes, 0, 0, tiled=True)


def assimilate(
    control,
    diffusivity,
    prof_tile,
    prof_cell,
    obs_prof,
    obs_field,
    obs_level,
    obs_weight,
    innovation,
    obs_precision,
):
    fields, _, ny, nx = control.shape
    tile = (ny, nx)
    profiles = prof_tile.shape[0]
    holders = lax.axis_size("gx") * lax.axis_size("gy")
    levels = lax.axis_size("obs")
    ext = ny + 2 * ROWS
    ctl = control.reshape(fields, ny, nx)
    rate = diffusivity.reshape(2, ny, nx)
    holder = prof_tile.reshape(1, profiles)
    cell = prof_cell.reshape(1, profiles)
    obs = [
        x.reshape(4, 128)
        for x in (obs_prof, obs_field, obs_level, obs_weight, innovation, obs_precision)
    ]
    planes = pltpu.VMEM((fields + 1, ext + 2 * PAD, nx), F32)
    coefs = (ext // 8, 5 * (fields + 1), 8, nx)

    given = [
        pltpu.with_memory_space_constraint(x, pltpu.HBM)
        for x in (ctl, rate, holder, cell, *obs)
    ]
    east, west, rows, own, rate, holder, cell, *obs = call(
        pack_inputs,
        [tile, tile, (levels * 16, 128), ctl.shape]
        + [jax.ShapeDtypeStruct(x.shape, x.dtype) for x in given[1:]],
        given,
        [pltpu.VMEM(ctl.shape, F32), pltpu.SemaphoreType.DMA((len(given),))],
        hbm=True,
    )
    left, right = pair(east, west, "gx")
    rows = exchange(rows, "obs")
    side = (fields + 3, ROWS, nx)
    strip, first, second = call(edges_first, [tile, side, side], [own, rate, left, right])
    first, second = swap(first, second, "gy")
    table, slots = call(
        tables, [(holders, 1, 384), (1, profiles)], [rows, holder, cell], flops=400_000_000
    )
    table = exchange(table, ("gx", "gy"))
    inc, coef = call(
        diffuse_control,
        [(fields, ny, nx), coefs],
        [own, rate, strip, first, second],
        [
            planes,
            planes,
            pltpu.VMEM((2, ext + 2 * PAD, nx), F32),
            planes,
        ],
        flops=40_000_000,
    )
    found, tab = call(
        gather,
        [(levels * fields * 8, 128), (136, 128)],
        [inc, table],
        [pltpu.VMEM((fields * 8, 128), F32)],
        flops=400_000_000,
    )
    found = exchange(found, "obs")
    pulled, east, west, columns = call(
        scatter,
        [(fields, ny, nx), tile, tile, (holders, 4, 128)],
        [found, tab],
        flops=400_000_000,
    )
    left, right = pair(east, west, "gx")
    columns = exchange(columns, ("gx", "gy"))
    side = (fields + 1, ROWS, nx)
    strip, first, second = call(edges_second, [tile, side, side], [pulled, left, right])
    first, second = swap(first, second, "gy")
    (gradient,) = call(
        diffuse_pulled,
        [(fields, ny, nx)],
        [pulled, strip, first, second, coef, own],
        [planes, planes],
        flops=40_000_000,
    )
    (departures,) = call(depart, [(4, 128)], [columns, holder, slots, *obs], flops=400_000_000)
    return gradient.reshape(control.shape), departures.reshape(obs_prof.shape)


def solution(mesh):
    in_specs = (
        P(None, "obs", "gy", "gx"),
        P(None, "obs", "gy", "gx"),
        P(("gx", "gy"), None),
        P(("gx", "gy")),
        P(("gx", "gy", "obs")),
        P(("gx", "gy", "obs")),
        P(("gx", "gy", "obs")),
        P(("gx", "gy", "obs")),
        P(("gx", "gy", "obs")),
        P(("gx", "gy", "obs")),
    )
    out_specs = (P(None, "obs", "gy", "gx"), P(("gx", "gy", "obs")))
    return jax.shard_map(
        assimilate, mesh=mesh, in_specs=in_specs, out_specs=out_specs, check_vma=False
    )
```

profile of v0, /device:TPU:32, one launch (start us, length us, event | category | flops | bytes accessed | tf_op | source)
XLA Modules:
  0.0 96.0 jit_solution(11058423748310558976)
XLA Ops:
  0.6 1.3 %shard_map.113 = (f32[128,128]{1,0:T(8,128)S(1)}, f32[128,128]{1,0:T(8,128)S(1)}, f32[128,128]{1,0:T(8,128)S(1)}, f32[4,128,128]{2,1,0:T(8,128)S(1)}, f32[2,128,...) custom-call(f32[4,128,128]{2,1,0:T(8,128)} %bitcast.23, ...), custom_call_target="tpu_custom_call" | custom-call | flops 1000000 | bytes 1015808 | tf_op jit(solution)/shard_map/pallas_call | solution.py:49
  1.9 18.5 %all_to_all.32 = f32[8,16,128]{2,1,0:T(8,128)S(1)} all-to-all(f32[8,16,128]{2,1,0:T(8,128)S(1)} %bitcast.20), channel_id=1, replica_groups=mesh['gx'=8,'gy'=8,'obs'=8] {'obs'}, dimensions={0} | all-to-all | bytes 131072 | tf_op jit(solution)/shard_map/all_to_all | solution.py:475
  20.4 2.6 %shard_map.116 = (f32[64,1,384]{2,1,0:T(1,128)}, f32[1,512]{1,0:T(1,128)S(1)}) custom-call(f32[128,128]{1,0:T(8,128)S(1)} %bitcast.21, s32[1,512]{1,0:T(1,128)S(1)} %get-tuple-element.40.holder, s32[1,512]{1,0:T(1,128)S(1)} %get-tuple-element.41.cell), custom_call_target="tpu_custom_call" | custom-call | flops 400000000 | bytes 169984 | tf_op jit(solution)/shard_map/pallas_call | solution.py:49
  23.0 10.2 %all-to-all-start.1 = ((f32[64,1,384]{2,1,0:T(1,128)}), f32[64,1,384]{2,1,0:T(1,128)S(1)}, u32[]{:S(2)}, u32[]{:S(2)}) async-start(f32[64,1,384]{2,1,0:T(1,128)} %get-tuple-element.42), calls=%async_computation.1 | async-start | bytes 196608 | tf_op jit(solution)/shard_map/all_to_all | solution.py:475
  33.2 0.1 collective-permute-start
  33.4 2.8 %collective-permute-start.1 = (f32[128,128]{1,0:T(8,128)S(1)}, f32[128,128]{1,0:T(8,128)S(1)}, u32[]{:S(2)}, u32[]{:S(2)}) collective-permute-start(f32[128,128]{1,0:T(8,128)S(1)} %get-tuple-element.34), channel_id=1, source_target_pairs={{0,448},{64,0},{128,64},{192,128},{256,192},{320,256},{384,320},{4... | collective-permute-start | bytes 196616 | tf_op jit(solution)/shard_map/ppermute | solution.py:461
  36.2 2.7 %collective-permute-done.left = f32[128,128]{1,0:T(8,128)S(1)} collective-permute-done((f32[128,128]{1,0:T(8,128)S(1)}, f32[128,128]{1,0:T(8,128)S(1)}, u32[]{:S(2)}, u32[]{:S(2)}) %collective-permute-start) | collective-permute-done | bytes 65568 | tf_op jit(solution)/shard_map/ppermute | solution.py:460
  38.9 0.0 collective-permute-done.1.right
  38.9 2.2 %collective-permute-start.2 = (f32[7,16,128]{2,1,0:T(8,128)S(1)}, f32[7,16,128]{2,1,0:T(8,128)S(1)}, u32[]{:S(2)}, u32[]{:S(2)}) collective-permute-start(f32[7,16,128]{2,1,0:T(8,128)S(1)} %get-tuple-element.36), channel_id=1, source_target_pairs={{0,8},{8,0},{16,24},{24,16},{32,40},{40,32},{48,56},{56,48},{1,9},... | collective-permute-start | bytes 172040 | tf_op jit(solution)/shard_map/ppermute | solution.py:469
  41.1 2.3 %collective-permute-start.3 = (f32[7,16,128]{2,1,0:T(8,128)S(1)}, f32[7,16,128]{2,1,0:T(8,128)S(1)}, u32[]{:S(2)}, u32[]{:S(2)}) collective-permute-start(f32[7,16,128]{2,1,0:T(8,128)S(1)} %get-tuple-element.37), channel_id=1, source_target_pairs={{8,16},{16,8},{24,32},{32,24},{40,48},{48,40},{9,17},{17,9},{25,33... | collective-permute-start | bytes 172040 | tf_op jit(solution)/shard_map/ppermute | solution.py:470
  43.4 1.6 %collective-permute-done.2.first = f32[7,16,128]{2,1,0:T(8,128)S(1)} collective-permute-done((f32[7,16,128]{2,1,0:T(8,128)S(1)}, f32[7,16,128]{2,1,0:T(8,128)S(1)}, u32[]{:S(2)}, u32[]{:S(2)}) %collective-permute-start.2) | collective-permute-done | bytes 57376 | tf_op jit(solution)/shard_map/ppermute | solution.py:469
  45.0 3.4 %collective-permute-done.3.second = f32[7,16,128]{2,1,0:T(8,128)S(1)} collective-permute-done((f32[7,16,128]{2,1,0:T(8,128)S(1)}, f32[7,16,128]{2,1,0:T(8,128)S(1)}, u32[]{:S(2)}, u32[]{:S(2)}) %collective-permute-start.3) | collective-permute-done | bytes 57376 | tf_op jit(solution)/shard_map/ppermute | solution.py:470
  48.4 3.6 %shard_map.115 = (f32[4,128,128]{2,1,0:T(8,128)S(1)}, f32[20,25,8,128]{3,2,1,0:T(8,128)S(1)}) custom-call(f32[4,128,128]{2,1,0:T(8,128)S(1)} %get-tuple-element.31.own, f32[2,128,128]{2,1,0:T(8,128)S(1)} %get-tuple-element.32.rate, f32[128,128]{1,0:T(8,128)S(1)} %get-tuple-element.35.strip, f32[7,16,128]{2,1,0:T(8,128)S(1)} %collective-permute-done.2.first, ...), custom_call_target="tpu_custom_call" | custom-call | flops 40000000 | bytes 2883584 | tf_op jit(solution)/shard_map/pallas_call | solution.py:49
  52.0 0.0 all-to-all-done.1.sent
  52.0 0.8 shard_map.117
  52.8 11.5 %all_to_all.33 = f32[8,32,128]{2,1,0:T(8,128)S(1)} all-to-all(f32[8,32,128]{2,1,0:T(8,128)S(1)} %bitcast.19), channel_id=1, replica_groups=mesh['gx'=8,'gy'=8,'obs'=8] {'obs'}, dimensions={0} | all-to-all | bytes 262144 | tf_op jit(solution)/shard_map/all_to_all | solution.py:475
  64.3 1.8 %shard_map.118 = (f32[4,128,128]{2,1,0:T(8,128)S(1)}, f32[128,128]{1,0:T(8,128)S(1)}, f32[128,128]{1,0:T(8,128)S(1)}, f32[64,4,128]{2,1,0:T(4,128)}) custom-call(f32[256,128]{1,0:T(8,128)S(1)} %bitcast.18, f32[136,128]{1,0:T(8,128)S(1)} %get-tuple-element.44.tab), custom_call_target="tpu_custom_call" | custom-call | flops 400000000 | bytes 724992 | tf_op jit(solution)/shard_map/pallas_call | solution.py:49
  66.1 9.9 %all-to-all-start.3 = ((f32[64,4,128]{2,1,0:T(4,128)}), f32[64,4,128]{2,1,0:T(4,128)S(1)}, u32[]{:S(2)}, u32[]{:S(2)}) async-start(f32[64,4,128]{2,1,0:T(4,128)} %get-tuple-element.52), calls=%async_computation.3 | async-start | bytes 262144 | tf_op jit(solution)/shard_map/all_to_all | solution.py:475
  76.0 0.1 collective-permute-start.4
  76.2 2.8 %collective-permute-start.5 = (f32[128,128]{1,0:T(8,128)S(1)}, f32[128,128]{1,0:T(8,128)S(1)}, u32[]{:S(2)}, u32[]{:S(2)}) collective-permute-start(f32[128,128]{1,0:T(8,128)S(1)} %get-tuple-element.47), channel_id=1, source_target_pairs={{0,448},{64,0},{128,64},{192,128},{256,192},{320,256},{384,320},{4... | collective-permute-start | bytes 196616 | tf_op jit(solution)/shard_map/ppermute | solution.py:461
  79.0 2.6 %collective-permute-done.4.left = f32[128,128]{1,0:T(8,128)S(1)} collective-permute-done((f32[128,128]{1,0:T(8,128)S(1)}, f32[128,128]{1,0:T(8,128)S(1)}, u32[]{:S(2)}, u32[]{:S(2)}) %collective-permute-start.4) | collective-permute-done | bytes 65568 | tf_op jit(solution)/shard_map/ppermute | solution.py:460
  81.6 0.0 collective-permute-done.5.right
  81.6 2.4 %collective-permute-start.6 = (f32[5,16,128]{2,1,0:T(8,128)S(1)}, f32[5,16,128]{2,1,0:T(8,128)S(1)}, u32[]{:S(2)}, u32[]{:S(2)}) collective-permute-start(f32[5,16,128]{2,1,0:T(8,128)S(1)} %get-tuple-element.49), channel_id=1, source_target_pairs={{0,8},{8,0},{16,24},{24,16},{32,40},{40,32},{48,56},{56,48},{1,9},... | collective-permute-start | bytes 122888 | tf_op jit(solution)/shard_map/ppermute | solution.py:469
  84.0 2.3 %collective-permute-start.7 = (f32[5,16,128]{2,1,0:T(8,128)S(1)}, f32[5,16,128]{2,1,0:T(8,128)S(1)}, u32[]{:S(2)}, u32[]{:S(2)}) collective-permute-start(f32[5,16,128]{2,1,0:T(8,128)S(1)} %get-tuple-element.50), channel_id=1, source_target_pairs={{8,16},{16,8},{24,32},{32,24},{40,48},{48,40},{9,17},{17,9},{25,33... | collective-permute-start | bytes 122888 | tf_op jit(solution)/shard_map/ppermute | solution.py:470
  86.3 1.2 %collective-permute-done.6.first = f32[5,16,128]{2,1,0:T(8,128)S(1)} collective-permute-done((f32[5,16,128]{2,1,0:T(8,128)S(1)}, f32[5,16,128]{2,1,0:T(8,128)S(1)}, u32[]{:S(2)}, u32[]{:S(2)}) %collective-permute-start.6) | collective-permute-done | bytes 40992 | tf_op jit(solution)/shard_map/ppermute | solution.py:469
  87.5 3.6 %collective-permute-done.7.second = f32[5,16,128]{2,1,0:T(8,128)S(1)} collective-permute-done((f32[5,16,128]{2,1,0:T(8,128)S(1)}, f32[5,16,128]{2,1,0:T(8,128)S(1)}, u32[]{:S(2)}, u32[]{:S(2)}) %collective-permute-start.7) | collective-permute-done | bytes 40992 | tf_op jit(solution)/shard_map/ppermute | solution.py:470
  91.1 3.4 %shard_map.120 = f32[4,128,128]{2,1,0:T(8,128)} custom-call(f32[4,128,128]{2,1,0:T(8,128)S(1)} %get-tuple-element.45.pulled, f32[128,128]{1,0:T(8,128)S(1)} %get-tuple-element.48.strip, f32[5,16,128]{2,1,0:T(8,128)S(1)} %collective-permute-done.6.first, f32[5,16,128]{2,1,0:T(8,128)S(1)} %collective-permute-done.7.second, ...), custom_call_target="tpu_custom_call" | custom-call | flops 40000000 | bytes 2981888 | tf_op jit(solution)/shard_map/pallas_call | solution.py:49
  94.5 0.0 all-to-all-done.3.columns
  94.6 1.4 %shard_map.121 = f32[4,128]{1,0:T(4,128)} custom-call(f32[64,4,128]{2,1,0:T(4,128)S(1)} %all-to-all-done.3.columns, s32[1,512]{1,0:T(1,128)S(1)} %get-tuple-element.40.holder, f32[1,512]{1,0:T(1,128)S(1)} %get-tuple-element.53.slots, s32[4,128]{1,0:T(4,128)S(1)} %get-tuple-element.54.prof, s32[4,128]{1,0:T(4,128)S(1)} %get-tuple-element.55.field, ...), custom_call_target="tpu_custom_call" | custom-call | flops 400000000 | bytes 149504 | tf_op jit(solution)/shard_map/pallas_call | solution.py:49
  (2 shorter events, 0.0 us)
Async XLA Ops:
  23.0 29.0 %all-to-all-start.1 = ((f32[64,1,384]{2,1,0:T(1,128)}), f32[64,1,384]{2,1,0:T(1,128)S(1)}, u32[]{:S(2)}, u32[]{:S(2)}) async-start(f32[64,1,384]{2,1,0:T(1,128)} %get-tuple-element.42), calls=%async_computation.1 | async-start | bytes 196608 | tf_op jit(solution)/shard_map/all_to_all | solution.py:475
  33.2 5.7 %collective-permute-start = (f32[128,128]{1,0:T(8,128)S(1)}, f32[128,128]{1,0:T(8,128)S(1)}, u32[]{:S(2)}, u32[]{:S(2)}) collective-permute-start(f32[128,128]{1,0:T(8,128)S(1)} %get-tuple-element.33), channel_id=1, source_target_pairs={{0,64},{64,128},{128,192},{192,256},{256,320},{320,384},{384,448},... | collective-permute-start | bytes 196616 | tf_op jit(solution)/shard_map/ppermute | solution.py:460
  33.4 5.5 %collective-permute-start.1 = (f32[128,128]{1,0:T(8,128)S(1)}, f32[128,128]{1,0:T(8,128)S(1)}, u32[]{:S(2)}, u32[]{:S(2)}) collective-permute-start(f32[128,128]{1,0:T(8,128)S(1)} %get-tuple-element.34), channel_id=1, source_target_pairs={{0,448},{64,0},{128,64},{192,128},{256,192},{320,256},{384,320},{4... | collective-permute-start | bytes 196616 | tf_op jit(solution)/shard_map/ppermute | solution.py:461
  38.9 6.1 %collective-permute-start.2 = (f32[7,16,128]{2,1,0:T(8,128)S(1)}, f32[7,16,128]{2,1,0:T(8,128)S(1)}, u32[]{:S(2)}, u32[]{:S(2)}) collective-permute-start(f32[7,16,128]{2,1,0:T(8,128)S(1)} %get-tuple-element.36), channel_id=1, source_target_pairs={{0,8},{8,0},{16,24},{24,16},{32,40},{40,32},{48,56},{56,48},{1,9},... | collective-permute-start | bytes 172040 | tf_op jit(solution)/shard_map/ppermute | solution.py:469
  41.1 7.3 %collective-permute-start.3 = (f32[7,16,128]{2,1,0:T(8,128)S(1)}, f32[7,16,128]{2,1,0:T(8,128)S(1)}, u32[]{:S(2)}, u32[]{:S(2)}) collective-permute-start(f32[7,16,128]{2,1,0:T(8,128)S(1)} %get-tuple-element.37), channel_id=1, source_target_pairs={{8,16},{16,8},{24,32},{32,24},{40,48},{48,40},{9,17},{17,9},{25,33... | collective-permute-start | bytes 172040 | tf_op jit(solution)/shard_map/ppermute | solution.py:470
  66.1 28.4 %all-to-all-start.3 = ((f32[64,4,128]{2,1,0:T(4,128)}), f32[64,4,128]{2,1,0:T(4,128)S(1)}, u32[]{:S(2)}, u32[]{:S(2)}) async-start(f32[64,4,128]{2,1,0:T(4,128)} %get-tuple-element.52), calls=%async_computation.3 | async-start | bytes 262144 | tf_op jit(solution)/shard_map/all_to_all | solution.py:475
  76.0 5.5 %collective-permute-start.4 = (f32[128,128]{1,0:T(8,128)S(1)}, f32[128,128]{1,0:T(8,128)S(1)}, u32[]{:S(2)}, u32[]{:S(2)}) collective-permute-start(f32[128,128]{1,0:T(8,128)S(1)} %get-tuple-element.46), channel_id=1, source_target_pairs={{0,64},{64,128},{128,192},{192,256},{256,320},{320,384},{384,448},... | collective-permute-start | bytes 196616 | tf_op jit(solution)/shard_map/ppermute | solution.py:460
  76.2 5.4 %collective-permute-start.5 = (f32[128,128]{1,0:T(8,128)S(1)}, f32[128,128]{1,0:T(8,128)S(1)}, u32[]{:S(2)}, u32[]{:S(2)}) collective-permute-start(f32[128,128]{1,0:T(8,128)S(1)} %get-tuple-element.47), channel_id=1, source_target_pairs={{0,448},{64,0},{128,64},{192,128},{256,192},{320,256},{384,320},{4... | collective-permute-start | bytes 196616 | tf_op jit(solution)/shard_map/ppermute | solution.py:461
  81.6 5.9 %collective-permute-start.6 = (f32[5,16,128]{2,1,0:T(8,128)S(1)}, f32[5,16,128]{2,1,0:T(8,128)S(1)}, u32[]{:S(2)}, u32[]{:S(2)}) collective-permute-start(f32[5,16,128]{2,1,0:T(8,128)S(1)} %get-tuple-element.49), channel_id=1, source_target_pairs={{0,8},{8,0},{16,24},{24,16},{32,40},{40,32},{48,56},{56,48},{1,9},... | collective-permute-start | bytes 122888 | tf_op jit(solution)/shard_map/ppermute | solution.py:469
  84.0 7.1 %collective-permute-start.7 = (f32[5,16,128]{2,1,0:T(8,128)S(1)}, f32[5,16,128]{2,1,0:T(8,128)S(1)}, u32[]{:S(2)}, u32[]{:S(2)}) collective-permute-start(f32[5,16,128]{2,1,0:T(8,128)S(1)} %get-tuple-element.50), channel_id=1, source_target_pairs={{8,16},{16,8},{24,32},{32,24},{40,48},{48,40},{9,17},{17,9},{25,33... | collective-permute-start | bytes 122888 | tf_op jit(solution)/shard_map/ppermute | solution.py:470
where the time goes:
time: 96.4 us; the launch traced here: 96 us
  starting transfers between devices  35.2 us (37%)
  blocking collectives  30 us (31%)
  waiting for transfers between devices  15.1 us (16%)
  Pallas kernels  15 us (16%)
    all_to_all x2, blocking collectives, exchange(): return lax.all_to_all(x, axes, 0, 0, tiled=True)  30 us
    all_to_all x2, starting transfers between devices, exchange(): return lax.all_to_all(x, axes, 0, 0, tiled=True)  20.1 us
    pallas_call x9, Pallas kernels, call(): pl.pallas_call(body, out_shape=outs, in_specs=[given] * len(args), out_sp...  15 us
    ppermute x2, waiting for transfers between devices, swap(): second = lax.ppermute(second, axis, high)  7.04 us
    ppermute x2, starting transfers between devices, pair(): lax.ppermute(back, axis, ring(axis, -1))  5.67 us
    ppermute x2, waiting for transfers between devices, pair(): lax.ppermute(forward, axis, ring(axis, 1))  5.27 us
    ppermute x2, starting transfers between devices, swap(): first = lax.ppermute(first, axis, low)  4.6 us
    ppermute x2, starting transfers between devices, swap(): second = lax.ppermute(second, axis, high)  4.52 us
  transfers between devices with their start and end apart: 10, of which 6 were waited for; matrix products, arithmetic and copies ran while one was open for 0% of the time, Pallas kernels for 7%

commit v1 on v0

--- a/solution.py
+++ b/solution.py
@@ -266,7 +266,7 @@
 
     each(coef.shape[0] * 8 // size, turned)
     ten_steps(a, b, coef)
-    size = 64
+    size = 128
 
     def back(block):
         for f in range(fields):
@@ -280,7 +280,7 @@
     fields, height, width = pulled.shape
     load_field(a, b, pulled, strip, first, second, fields)
     ten_steps(a, b, coef)
-    size = 64
+    size = 128
 
     def back(block):
         for f in range(fields):
@@ -438,7 +438,8 @@
     hot = jnp.concatenate(
         [one_hot(subs((profiles, 128)) == prof[pl.ds(c, 1), :]) for c in range(4)], axis=1
     )
-    seen = sum(dot_nn(part, hot) for part in split3(values))
+    seen = dot_nn(jnp.concatenate(split3(values), axis=0), hot)
+    seen = seen[0:32] + seen[32:64] + seen[64:96]
     row = subs((32, 128))
     for c in range(4):
         at = pl.ds(c, 1)
@@ -466,9 +467,7 @@
     count = lax.axis_size(axis)
     low = [(i, i ^ 1) for i in range(count)]
     high = [(i, (i + 1 ^ 1) - 1) for i in range(1, count - 1)]
-    first = lax.ppermute(first, axis, low)
-    second = lax.ppermute(second, axis, high)
-    return first, second
+    return lax.ppermute(first, axis, low), lax.ppermute(second, axis, high)
 
 
 def exchange(x, axes):

time: 96.4 us -> 96 us (level)
  no operation moved by 1% of the time
where the time goes in v1:
time: 96 us; the launch traced here: 95.7 us
  starting transfers between devices  35.2 us (37%)
  blocking collectives  30 us (31%)
  waiting for transfers between devices  15.1 us (16%)
  Pallas kernels  14.6 us (15%)
    all_to_all x2, blocking collectives, exchange(): return lax.all_to_all(x, axes, 0, 0, tiled=True)  30 us
    all_to_all x2, starting transfers between devices, exchange(): return lax.all_to_all(x, axes, 0, 0, tiled=True)  20.1 us
    pallas_call x9, Pallas kernels, call(): pl.pallas_call(body, out_shape=outs, in_specs=[given] * len(args), out_sp...  14.6 us
    ppermute x4, waiting for transfers between devices, swap(): return (lax.ppermute(first, axis, low), lax.ppermute(second, axis, high))  9.86 us
    ppermute x4, starting transfers between devices, swap(): return (lax.ppermute(first, axis, low), lax.ppermute(second, axis, high))  9.12 us
    ppermute x2, starting transfers between devices, pair(): lax.ppermute(back, axis, ring(axis, -1))  5.67 us
    ppermute x2, waiting for transfers between devices, pair(): lax.ppermute(forward, axis, ring(axis, 1))  5.27 us
  transfers between devices with their start and end apart: 10, of which 6 were waited for; matrix products, arithmetic and copies ran while one was open for 0% of the time, Pallas kernels for 7%

profile of v1, /device:TPU:32, one launch (start us, length us, event | category | flops | bytes accessed | tf_op | source)
XLA Modules:
  0.0 95.7 jit_solution(10690403476836484514)
XLA Ops:
  0.6 1.3 %shard_map.113 = (f32[128,128]{1,0:T(8,128)S(1)}, f32[128,128]{1,0:T(8,128)S(1)}, f32[128,128]{1,0:T(8,128)S(1)}, f32[4,128,128]{2,1,0:T(8,128)S(1)}, f32[2,128,...) custom-call(f32[4,128,128]{2,1,0:T(8,128)} %bitcast.23, ...), custom_call_target="tpu_custom_call" | custom-call | flops 1000000 | bytes 1015808 | tf_op jit(solution)/shard_map/pallas_call | solution.py:49
  1.9 18.5 %all_to_all.32 = f32[8,16,128]{2,1,0:T(8,128)S(1)} all-to-all(f32[8,16,128]{2,1,0:T(8,128)S(1)} %bitcast.20), channel_id=1, replica_groups=mesh['gx'=8,'gy'=8,'obs'=8] {'obs'}, dimensions={0} | all-to-all | bytes 131072 | tf_op jit(solution)/shard_map/all_to_all | solution.py:474
  20.4 2.6 %shard_map.116 = (f32[64,1,384]{2,1,0:T(1,128)}, f32[1,512]{1,0:T(1,128)S(1)}) custom-call(f32[128,128]{1,0:T(8,128)S(1)} %bitcast.21, s32[1,512]{1,0:T(1,128)S(1)} %get-tuple-element.40.holder, s32[1,512]{1,0:T(1,128)S(1)} %get-tuple-element.41.cell), custom_call_target="tpu_custom_call" | custom-call | flops 400000000 | bytes 169984 | tf_op jit(solution)/shard_map/pallas_call | solution.py:49
  23.0 10.2 %all-to-all-start.1 = ((f32[64,1,384]{2,1,0:T(1,128)}), f32[64,1,384]{2,1,0:T(1,128)S(1)}, u32[]{:S(2)}, u32[]{:S(2)}) async-start(f32[64,1,384]{2,1,0:T(1,128)} %get-tuple-element.42), calls=%async_computation.1 | async-start | bytes 196608 | tf_op jit(solution)/shard_map/all_to_all | solution.py:474
  33.2 0.1 collective-permute-start
  33.4 2.8 %collective-permute-start.1 = (f32[128,128]{1,0:T(8,128)S(1)}, f32[128,128]{1,0:T(8,128)S(1)}, u32[]{:S(2)}, u32[]{:S(2)}) collective-permute-start(f32[128,128]{1,0:T(8,128)S(1)} %get-tuple-element.34), channel_id=1, source_target_pairs={{0,448},{64,0},{128,64},{192,128},{256,192},{320,256},{384,320},{4... | collective-permute-start | bytes 196616 | tf_op jit(solution)/shard_map/ppermute | solution.py:462
  36.2 2.7 %collective-permute-done.left = f32[128,128]{1,0:T(8,128)S(1)} collective-permute-done((f32[128,128]{1,0:T(8,128)S(1)}, f32[128,128]{1,0:T(8,128)S(1)}, u32[]{:S(2)}, u32[]{:S(2)}) %collective-permute-start) | collective-permute-done | bytes 65568 | tf_op jit(solution)/shard_map/ppermute | solution.py:461
  38.9 0.0 collective-permute-done.1.right
  38.9 2.2 %collective-permute-start.2 = (f32[7,16,128]{2,1,0:T(8,128)S(1)}, f32[7,16,128]{2,1,0:T(8,128)S(1)}, u32[]{:S(2)}, u32[]{:S(2)}) collective-permute-start(f32[7,16,128]{2,1,0:T(8,128)S(1)} %get-tuple-element.36), channel_id=1, source_target_pairs={{0,8},{8,0},{16,24},{24,16},{32,40},{40,32},{48,56},{56,48},{1,9},... | collective-permute-start | bytes 172040 | tf_op jit(solution)/shard_map/ppermute | solution.py:470
  41.1 2.3 %collective-permute-start.3 = (f32[7,16,128]{2,1,0:T(8,128)S(1)}, f32[7,16,128]{2,1,0:T(8,128)S(1)}, u32[]{:S(2)}, u32[]{:S(2)}) collective-permute-start(f32[7,16,128]{2,1,0:T(8,128)S(1)} %get-tuple-element.37), channel_id=1, source_target_pairs={{8,16},{16,8},{24,32},{32,24},{40,48},{48,40},{9,17},{17,9},{25,33... | collective-permute-start | bytes 172040 | tf_op jit(solution)/shard_map/ppermute | solution.py:470
  43.4 1.6 %collective-permute-done.2.first = f32[7,16,128]{2,1,0:T(8,128)S(1)} collective-permute-done((f32[7,16,128]{2,1,0:T(8,128)S(1)}, f32[7,16,128]{2,1,0:T(8,128)S(1)}, u32[]{:S(2)}, u32[]{:S(2)}) %collective-permute-start.2) | collective-permute-done | bytes 57376 | tf_op jit(solution)/shard_map/ppermute | solution.py:470
  45.0 3.4 %collective-permute-done.3.second = f32[7,16,128]{2,1,0:T(8,128)S(1)} collective-permute-done((f32[7,16,128]{2,1,0:T(8,128)S(1)}, f32[7,16,128]{2,1,0:T(8,128)S(1)}, u32[]{:S(2)}, u32[]{:S(2)}) %collective-permute-start.3) | collective-permute-done | bytes 57376 | tf_op jit(solution)/shard_map/ppermute | solution.py:470
  48.4 3.5 %shard_map.115 = (f32[4,128,128]{2,1,0:T(8,128)S(1)}, f32[20,25,8,128]{3,2,1,0:T(8,128)S(1)}) custom-call(f32[4,128,128]{2,1,0:T(8,128)S(1)} %get-tuple-element.31.own, f32[2,128,128]{2,1,0:T(8,128)S(1)} %get-tuple-element.32.rate, f32[128,128]{1,0:T(8,128)S(1)} %get-tuple-element.35.strip, f32[7,16,128]{2,1,0:T(8,128)S(1)} %collective-permute-done.2.first, ...), custom_call_target="tpu_custom_call" | custom-call | flops 40000000 | bytes 2883584 | tf_op jit(solution)/shard_map/pallas_call | solution.py:49
  51.9 0.0 all-to-all-done.1.sent
  51.9 0.8 shard_map.117
  52.8 11.5 %all_to_all.33 = f32[8,32,128]{2,1,0:T(8,128)S(1)} all-to-all(f32[8,32,128]{2,1,0:T(8,128)S(1)} %bitcast.19), channel_id=1, replica_groups=mesh['gx'=8,'gy'=8,'obs'=8] {'obs'}, dimensions={0} | all-to-all | bytes 262144 | tf_op jit(solution)/shard_map/all_to_all | solution.py:474
  64.2 1.8 %shard_map.118 = (f32[4,128,128]{2,1,0:T(8,128)S(1)}, f32[128,128]{1,0:T(8,128)S(1)}, f32[128,128]{1,0:T(8,128)S(1)}, f32[64,4,128]{2,1,0:T(4,128)}) custom-call(f32[256,128]{1,0:T(8,128)S(1)} %bitcast.18, f32[136,128]{1,0:T(8,128)S(1)} %get-tuple-element.44.tab), custom_call_target="tpu_custom_call" | custom-call | flops 400000000 | bytes 724992 | tf_op jit(solution)/shard_map/pallas_call | solution.py:49
  66.1 9.9 %all-to-all-start.3 = ((f32[64,4,128]{2,1,0:T(4,128)}), f32[64,4,128]{2,1,0:T(4,128)S(1)}, u32[]{:S(2)}, u32[]{:S(2)}) async-start(f32[64,4,128]{2,1,0:T(4,128)} %get-tuple-element.52), calls=%async_computation.3 | async-start | bytes 262144 | tf_op jit(solution)/shard_map/all_to_all | solution.py:474
  76.0 0.1 collective-permute-start.4
  76.1 2.8 %collective-permute-start.5 = (f32[128,128]{1,0:T(8,128)S(1)}, f32[128,128]{1,0:T(8,128)S(1)}, u32[]{:S(2)}, u32[]{:S(2)}) collective-permute-start(f32[128,128]{1,0:T(8,128)S(1)} %get-tuple-element.47), channel_id=1, source_target_pairs={{0,448},{64,0},{128,64},{192,128},{256,192},{320,256},{384,320},{4... | collective-permute-start | bytes 196616 | tf_op jit(solution)/shard_map/ppermute | solution.py:462
  78.9 2.6 %collective-permute-done.4.left = f32[128,128]{1,0:T(8,128)S(1)} collective-permute-done((f32[128,128]{1,0:T(8,128)S(1)}, f32[128,128]{1,0:T(8,128)S(1)}, u32[]{:S(2)}, u32[]{:S(2)}) %collective-permute-start.4) | collective-permute-done | bytes 65568 | tf_op jit(solution)/shard_map/ppermute | solution.py:461
  81.5 0.0 collective-permute-done.5.right
  81.5 2.4 %collective-permute-start.6 = (f32[5,16,128]{2,1,0:T(8,128)S(1)}, f32[5,16,128]{2,1,0:T(8,128)S(1)}, u32[]{:S(2)}, u32[]{:S(2)}) collective-permute-start(f32[5,16,128]{2,1,0:T(8,128)S(1)} %get-tuple-element.49), channel_id=1, source_target_pairs={{0,8},{8,0},{16,24},{24,16},{32,40},{40,32},{48,56},{56,48},{1,9},... | collective-permute-start | bytes 122888 | tf_op jit(solution)/shard_map/ppermute | solution.py:470
  83.9 2.3 %collective-permute-start.7 = (f32[5,16,128]{2,1,0:T(8,128)S(1)}, f32[5,16,128]{2,1,0:T(8,128)S(1)}, u32[]{:S(2)}, u32[]{:S(2)}) collective-permute-start(f32[5,16,128]{2,1,0:T(8,128)S(1)} %get-tuple-element.50), channel_id=1, source_target_pairs={{8,16},{16,8},{24,32},{32,24},{40,48},{48,40},{9,17},{17,9},{25,33... | collective-permute-start | bytes 122888 | tf_op jit(solution)/shard_map/ppermute | solution.py:470
  86.2 1.2 %collective-permute-done.6.first = f32[5,16,128]{2,1,0:T(8,128)S(1)} collective-permute-done((f32[5,16,128]{2,1,0:T(8,128)S(1)}, f32[5,16,128]{2,1,0:T(8,128)S(1)}, u32[]{:S(2)}, u32[]{:S(2)}) %collective-permute-start.6) | collective-permute-done | bytes 40992 | tf_op jit(solution)/shard_map/ppermute | solution.py:470
  87.4 3.6 %collective-permute-done.7.second = f32[5,16,128]{2,1,0:T(8,128)S(1)} collective-permute-done((f32[5,16,128]{2,1,0:T(8,128)S(1)}, f32[5,16,128]{2,1,0:T(8,128)S(1)}, u32[]{:S(2)}, u32[]{:S(2)}) %collective-permute-start.7) | collective-permute-done | bytes 40992 | tf_op jit(solution)/shard_map/ppermute | solution.py:470
  91.0 3.3 %shard_map.120 = f32[4,128,128]{2,1,0:T(8,128)} custom-call(f32[4,128,128]{2,1,0:T(8,128)S(1)} %get-tuple-element.45.pulled, f32[128,128]{1,0:T(8,128)S(1)} %get-tuple-element.48.strip, f32[5,16,128]{2,1,0:T(8,128)S(1)} %collective-permute-done.6.first, f32[5,16,128]{2,1,0:T(8,128)S(1)} %collective-permute-done.7.second, ...), custom_call_target="tpu_custom_call" | custom-call | flops 40000000 | bytes 2981888 | tf_op jit(solution)/shard_map/pallas_call | solution.py:49
  94.4 0.0 all-to-all-done.3.columns
  94.4 1.3 %shard_map.121 = f32[4,128]{1,0:T(4,128)} custom-call(f32[64,4,128]{2,1,0:T(4,128)S(1)} %all-to-all-done.3.columns, s32[1,512]{1,0:T(1,128)S(1)} %get-tuple-element.40.holder, f32[1,512]{1,0:T(1,128)S(1)} %get-tuple-element.53.slots, s32[4,128]{1,0:T(4,128)S(1)} %get-tuple-element.54.prof, s32[4,128]{1,0:T(4,128)S(1)} %get-tuple-element.55.field, ...), custom_call_target="tpu_custom_call" | custom-call | flops 400000000 | bytes 149504 | tf_op jit(solution)/shard_map/pallas_call | solution.py:49
  (2 shorter events, 0.0 us)
Async XLA Ops:
  23.0 28.9 %all-to-all-start.1 = ((f32[64,1,384]{2,1,0:T(1,128)}), f32[64,1,384]{2,1,0:T(1,128)S(1)}, u32[]{:S(2)}, u32[]{:S(2)}) async-start(f32[64,1,384]{2,1,0:T(1,128)} %get-tuple-element.42), calls=%async_computation.1 | async-start | bytes 196608 | tf_op jit(solution)/shard_map/all_to_all | solution.py:474
  33.2 5.7 %collective-permute-start = (f32[128,128]{1,0:T(8,128)S(1)}, f32[128,128]{1,0:T(8,128)S(1)}, u32[]{:S(2)}, u32[]{:S(2)}) collective-permute-start(f32[128,128]{1,0:T(8,128)S(1)} %get-tuple-element.33), channel_id=1, source_target_pairs={{0,64},{64,128},{128,192},{192,256},{256,320},{320,384},{384,448},... | collective-permute-start | bytes 196616 | tf_op jit(solution)/shard_map/ppermute | solution.py:461
  33.4 5.5 %collective-permute-start.1 = (f32[128,128]{1,0:T(8,128)S(1)}, f32[128,128]{1,0:T(8,128)S(1)}, u32[]{:S(2)}, u32[]{:S(2)}) collective-permute-start(f32[128,128]{1,0:T(8,128)S(1)} %get-tuple-element.34), channel_id=1, source_target_pairs={{0,448},{64,0},{128,64},{192,128},{256,192},{320,256},{384,320},{4... | collective-permute-start | bytes 196616 | tf_op jit(solution)/shard_map/ppermute | solution.py:462
  38.9 6.1 %collective-permute-start.2 = (f32[7,16,128]{2,1,0:T(8,128)S(1)}, f32[7,16,128]{2,1,0:T(8,128)S(1)}, u32[]{:S(2)}, u32[]{:S(2)}) collective-permute-start(f32[7,16,128]{2,1,0:T(8,128)S(1)} %get-tuple-element.36), channel_id=1, source_target_pairs={{0,8},{8,0},{16,24},{24,16},{32,40},{40,32},{48,56},{56,48},{1,9},... | collective-permute-start | bytes 172040 | tf_op jit(solution)/shard_map/ppermute | solution.py:470
  41.1 7.3 %collective-permute-start.3 = (f32[7,16,128]{2,1,0:T(8,128)S(1)}, f32[7,16,128]{2,1,0:T(8,128)S(1)}, u32[]{:S(2)}, u32[]{:S(2)}) collective-permute-start(f32[7,16,128]{2,1,0:T(8,128)S(1)} %get-tuple-element.37), channel_id=1, source_target_pairs={{8,16},{16,8},{24,32},{32,24},{40,48},{48,40},{9,17},{17,9},{25,33... | collective-permute-start | bytes 172040 | tf_op jit(solution)/shard_map/ppermute | solution.py:470
  66.1 28.3 %all-to-all-start.3 = ((f32[64,4,128]{2,1,0:T(4,128)}), f32[64,4,128]{2,1,0:T(4,128)S(1)}, u32[]{:S(2)}, u32[]{:S(2)}) async-start(f32[64,4,128]{2,1,0:T(4,128)} %get-tuple-element.52), calls=%async_computation.3 | async-start | bytes 262144 | tf_op jit(solution)/shard_map/all_to_all | solution.py:474
  76.0 5.5 %collective-permute-start.4 = (f32[128,128]{1,0:T(8,128)S(1)}, f32[128,128]{1,0:T(8,128)S(1)}, u32[]{:S(2)}, u32[]{:S(2)}) collective-permute-start(f32[128,128]{1,0:T(8,128)S(1)} %get-tuple-element.46), channel_id=1, source_target_pairs={{0,64},{64,128},{128,192},{192,256},{256,320},{320,384},{384,448},... | collective-permute-start | bytes 196616 | tf_op jit(solution)/shard_map/ppermute | solution.py:461
  76.1 5.4 %collective-permute-start.5 = (f32[128,128]{1,0:T(8,128)S(1)}, f32[128,128]{1,0:T(8,128)S(1)}, u32[]{:S(2)}, u32[]{:S(2)}) collective-permute-start(f32[128,128]{1,0:T(8,128)S(1)} %get-tuple-element.47), channel_id=1, source_target_pairs={{0,448},{64,0},{128,64},{192,128},{256,192},{320,256},{384,320},{4... | collective-permute-start | bytes 196616 | tf_op jit(solution)/shard_map/ppermute | solution.py:462
  81.5 5.9 %collective-permute-start.6 = (f32[5,16,128]{2,1,0:T(8,128)S(1)}, f32[5,16,128]{2,1,0:T(8,128)S(1)}, u32[]{:S(2)}, u32[]{:S(2)}) collective-permute-start(f32[5,16,128]{2,1,0:T(8,128)S(1)} %get-tuple-element.49), channel_id=1, source_target_pairs={{0,8},{8,0},{16,24},{24,16},{32,40},{40,32},{48,56},{56,48},{1,9},... | collective-permute-start | bytes 122888 | tf_op jit(solution)/shard_map/ppermute | solution.py:470
  83.9 7.1 %collective-permute-start.7 = (f32[5,16,128]{2,1,0:T(8,128)S(1)}, f32[5,16,128]{2,1,0:T(8,128)S(1)}, u32[]{:S(2)}, u32[]{:S(2)}) collective-permute-start(f32[5,16,128]{2,1,0:T(8,128)S(1)} %get-tuple-element.50), channel_id=1, source_target_pairs={{8,16},{16,8},{24,32},{32,24},{40,48},{48,40},{9,17},{17,9},{25,33... | collective-permute-start | bytes 122888 | tf_op jit(solution)/shard_map/ppermute | solution.py:470
